TPU v7x, 32 devices: a whole 2x2x4 slice. The times are simulated.
32 devices in a mesh: light: 4 (over z), pix: 4 (over x, core), cam: 2 (over y).
Axes of the slice: x: 2, y: 2, z: 4, core: 2. Of those that a mesh axis runs over, the one named last changes fastest.
Arguments:
- reflectance: bfloat16 [1024, 32, 4096], P('light', 'cam', 'pix'), may hold values from -120 to 120
- start_basis: float32 [1024, 128], replicated, may hold values from -6 to 6
Outputs:
- core_tensor: float32 [128, 32, 4096], P('light', 'cam', 'pix')
- light_basis: float32 [1024, 128], P('light')
All inputs are finite; a program needn't handle non-finite values.
Results may differ from a plain program's by a relative error of at most 0.015.
Values may be sent and summed in bfloat16 or wider, within the bound.
A program may use at most 128 MiB of HBM per device.

v0:
```python
import jax
import jax.numpy as jnp
from jax import lax
from jax.sharding import PartitionSpec as P

ITERS = 2


def orthonormal(image_full):
    inner_gram = jnp.dot(
        image_full.T,
        image_full,
        preferred_element_type=jnp.float32,
        precision=lax.Precision.HIGHEST,
    )
    factor = jnp.linalg.cholesky(inner_gram)
    return lax.linalg.triangular_solve(
        factor, image_full, left_side=False, lower=True, transpose_a=True
    )


def per_device(reflectance, start_basis):
    light_rows, camera_cols, pixels = reflectance.shape
    rank_total = start_basis.shape[1]
    light_count = lax.axis_size("light")
    position = lax.axis_index("light")
    inverse_cols = 1.0 / (camera_cols * pixels * lax.axis_size("cam") * lax.axis_size("pix"))
    fibers = reflectance.reshape(light_rows, camera_cols * pixels)
    full_gram = None
    exchanged = None
    exchanged = lax.all_to_all(reflectance, "light", split_axis=2, concat_axis=0, tiled=True)
    gathered = exchanged.reshape(light_rows * light_count, -1)
    own_gram = lax.dot_general(
        gathered, gathered, (((1,), (1,)), ((), ())), preferred_element_type=jnp.float32
    )
    full_gram = lax.psum(own_gram, ("light", "pix", "cam")) * inverse_cols
    gram_rows = lax.dynamic_slice_in_dim(full_gram, position * light_rows, light_rows, 0)
    basis_now = start_basis
    for iteration in range(ITERS):
        image_rows = jnp.dot(
            gram_rows,
            basis_now,
            preferred_element_type=jnp.float32,
            precision=lax.Precision.HIGHEST,
        )
        image_full = lax.all_gather(
            image_rows.astype(jnp.bfloat16), "light", axis=0, tiled=True
        ).astype(image_rows.dtype)
        basis_now = orthonormal(image_full)
    basis_rows = lax.dynamic_slice_in_dim(basis_now, position * light_rows, light_rows, 0)
    rank_rows = rank_total // light_count
    rounded = basis_rows.astype(jnp.bfloat16)
    core_rows = lax.psum_scatter(
        lax.dot_general(
            rounded, fibers, (((0,), (0,)), ((), ())), preferred_element_type=jnp.float32
        ).astype(jnp.bfloat16),
        "light",
        scatter_dimension=0,
        tiled=True,
    ).astype(jnp.float32)
    return (core_rows.reshape(rank_rows, camera_cols, pixels), basis_rows)


def solution(mesh):
    placed = (P("light", "cam", "pix"), P())
    return jax.shard_map(
        per_device,
        mesh=mesh,
        in_specs=placed,
        out_specs=(P("light", "cam", "pix"), P("light", None)),
        check_vma=False,
    )
```

profile of v0, /device:TPU:0, one launch (start us, length us, event | category | flops | bytes accessed | tf_op | source)
XLA Modules:
  0.0 573.0 jit_solution(15910480420709180516)
XLA Ops:
  7.2 13.4 %copy.16 = bf16[256,16,1024]{0,1,2:T(8,128)(2,1)} copy(bf16[256,16,1024]{2,1,0:T(8,128)(2,1)} %param.5) | data formatting | bytes 16777216 | tf_op args[0]
  20.7 192.2 %all_to_all.15 = bf16[256,16,1024]{0,1,2:T(8,128)(2,1)} all-to-all(bf16[256,16,1024]{0,1,2:T(8,128)(2,1)} %copy.16), channel_id=1, replica_groups=mesh['light'=4,'pix'=4,'cam'=2] {'light'}, dimensions={2} | all-to-all | bytes 16777216 | tf_op jit(solution)/shard_map/all_to_all | solution.py:31
  212.9 16.0 %copy.17 = bf16[256,16,4,256]{3,1,0,2:T(8,128)(2,1)} copy(bf16[256,16,4,256]{0,1,3,2:T(8,128)(2,1)} %bitcast.43) | data formatting | bytes 16777216 | tf_op jit(solution)/shard_map/all_to_all | solution.py:31
  228.9 12.2 %copy.21 = bf16[128,8,16,256]{3,1,2,0:T(8,128)(2,1)} copy(bf16[128,8,16,256]{3,2,1,0:T(8,128)(2,1)} %bitcast.44) | data formatting | bytes 16777216
  241.1 16.0 %fusion.17 = f32[1024,1024]{1,0:T(8,128)} fusion(bf16[1024,4096]{1,0:T(8,128)(2,1)} %bitcast.45), kind=kOutput, calls=%fused_computation.33 | convolution fusion | flops 8589934592 | bytes 12582912 | tf_op jit(solution)/shard_map/dot_general | solution.py:33
  257.7 15.6 %copy.22 = bf16[32,8,16,1024]{3,1,2,0:T(8,128)(2,1)} copy(bf16[32,8,16,1024]{3,2,1,0:T(8,128)(2,1)} %bitcast.41) | data formatting | bytes 16777216
  273.3 125.7 %all-reduce.2.cloned.1.call-done = f32[1024,1024]{1,0:T(8,128)} async-done(((f32[1024,1024]{1,0:T(8,128)}), f32[1024,1024]{1,0:T(8,128)}) %all-reduce.2.cloned.1.call-update) | async-done | bytes 4194320 | tf_op jit(solution)/shard_map/psum | solution.py:36
  399.0 2.2 convolution_convert_fusion.2
  401.2 14.5 %all_gather.6 = bf16[1024,128]{1,0:T(8,128)(2,1)S(1)} all-gather(bf16[256,128]{1,0:T(8,128)(2,1)S(1)} %convolution_convert_fusion.2), channel_id=1, replica_groups=mesh['light'=4,'pix'=4,'cam'=2] {'light'}, dimensions={0}, use_global_device_ids=true | all-gather | bytes 327680 | tf_op jit(solution)/shard_map/all_gather | solution.py:46
  416.1 11.7 %cholesky.44 = f32[128,128]{1,0:T(8,128)S(1)} custom-call(f32[128,128]{1,0:T(8,128)S(1)} %fusion.9), custom_call_target="Cholesky" | custom-call | tf_op jit(solution)/shard_map/jit(cholesky)/cholesky | solution.py:16
  427.9 0.6 compare_reduce_fusion.1
  428.5 0.7 fusion.4
  429.2 9.8 %custom-call.6 = f32[1,128,128]{1,2,0:T(8,128)S(1)} custom-call(f32[1,128,128]{2,1,0:T(8,128)S(1)} %fusion.4), custom_call_target="InvertDiagBlocksLowerTriangular" | custom-call | tf_op jit(solution)/shard_map/triangular_solve/custom-call.0 | solution.py:17
  439.6 2.2 convolution_convert_fusion.1
  441.8 14.5 %all_gather.7 = bf16[1024,128]{1,0:T(8,128)(2,1)S(1)} all-gather(bf16[256,128]{1,0:T(8,128)(2,1)S(1)} %convolution_convert_fusion.1), channel_id=1, replica_groups=mesh['light'=4,'pix'=4,'cam'=2] {'light'}, dimensions={0}, use_global_device_ids=true | all-gather | bytes 327680 | tf_op jit(solution)/shard_map/all_gather | solution.py:46
  456.7 11.7 %cholesky.55 = f32[128,128]{1,0:T(8,128)S(1)} custom-call(f32[128,128]{1,0:T(8,128)S(1)} %fusion.7), custom_call_target="Cholesky" | custom-call | tf_op jit(solution)/shard_map/jit(cholesky)/cholesky | solution.py:16
  468.4 0.6 compare_reduce_fusion
  469.1 0.7 fusion.5
  469.7 9.8 %custom-call.7 = f32[1,128,128]{1,2,0:T(8,128)S(1)} custom-call(f32[1,128,128]{2,1,0:T(8,128)S(1)} %fusion.5), custom_call_target="InvertDiagBlocksLowerTriangular" | custom-call | tf_op jit(solution)/shard_map/triangular_solve/custom-call.0 | solution.py:17
  479.6 0.6 convolution_bitcast_fusion
  480.2 6.6 %convolution_convert_fusion = bf16[128,16384]{1,0:T(8,128)(2,1)} fusion(bf16[256,16384]{1,0:T(8,128)(2,1)} %bitcast.42, f32[256,128]{0,1:T(8,128)S(1)} %constant_dynamic-slice_fusion), kind=kOutput, calls=%fused_computation | convolution fusion | flops 1075871744 | bytes 12713984 | tf_op jit(solution)/shard_map/dot_general | solution.py:54
  486.9 0.8 copy.20
  487.6 75.2 %reduce-scatter.2.cloned.1.call-done = bf16[32,16384]{1,0:T(8,128)(2,1)} async-done(((bf16[128,16384]{1,0:T(8,128)(2,1)}), bf16[32,16384]{1,0:T(8,128)(2,1)}) %reduce-scatter.2.cloned.1.call-update) | async-done | bytes 1048592 | tf_op jit(solution)/shard_map/reduce_scatter | solution.py:53
  562.8 3.2 copy.23
  (16 shorter events, 2.0 us)
Async XLA Ops:
  7.2 391.9 %copy-start = (f32[1024,128]{1,0:T(8,128)S(1)}, f32[1024,128]{1,0:T(8,128)}, u32[]{:S(2)}) copy-start(f32[1024,128]{1,0:T(8,128)} %param.6) | copy-start | bytes 1572868
  7.2 391.8 %all-reduce.2.cloned.1.call-start = ((), (), s32[]{:S(2)}) async-start(), calls=%async_computation.2 | async-start | bytes 8388608 | tf_op jit(solution)/shard_map/psum | solution.py:36
  257.1 305.7 %reduce-scatter.2.cloned.1.call-start = ((), (), s32[]{:S(2)}) async-start(), calls=%async_computation.3 | async-start | bytes 5242880 | tf_op jit(solution)/shard_map/reduce_scatter | solution.py:53
Sparse Core Ops, SparseCore 0:
  257.3 141.7 all-reduce.1
  487.0 75.7 reduce-scatter.1
where the time goes:
time: 582 us; the launch traced here: 573 us
  blocking collectives  221 us (38%)
  waiting for transfers between devices  201 us (35%)
  local copies, waits for them, and re-layouts  61.5 us (11%)
  other arithmetic  45.7 us (8%)
  matrix products  28.8 us (5%)
  between operations  14.4 us (2%)
    all_to_all x1, blocking collectives, per_device(): lax.all_to_all(reflectance, 'light', split_axis=2, concat_axis=0, tiled=T...  192 us
    psum x1, waiting for transfers between devices, per_device(): full_gram = lax.psum(own_gram, ('light', 'pix', 'cam')) * inverse_cols  126 us
    reduce_scatter x1, waiting for transfers between devices, per_device(): lax.psum_scatter(lax.dot_general(rounded, fibers, (((0,), (0,)), ((), ())...  75.2 us
    unnamed x7, local copies, waits for them, and re-layouts  45.2 us
    all_gather x2, blocking collectives, per_device(): lax.all_gather(image_rows.astype(jnp.bfloat16), 'light', axis=0, tiled=True)  28.9 us
    another operation x6, other arithmetic, orthonormal(): factor = jnp.linalg.cholesky(inner_gram)  24.8 us
    another operation x4, other arithmetic, orthonormal(): lax.linalg.triangular_solve(factor, image_full, left_side=False, lower=Tr...  20.9 us
    all_to_all x1, local copies, waits for them, and re-layouts, per_device(): lax.all_to_all(reflectance, 'light', split_axis=2, concat_axis=0, tiled=T...  16 us
  transfers between devices with their start and end apart: 2, of which 2 were waited for; matrix products, arithmetic and copies ran while one was open for 3% of the time, Pallas kernels for 0%

commit v1 on v0

--- a/solution.py
+++ b/solution.py
@@ -33,7 +33,7 @@
     own_gram = lax.dot_general(
         gathered, gathered, (((1,), (1,)), ((), ())), preferred_element_type=jnp.float32
     )
-    full_gram = lax.psum(own_gram, ("light", "pix", "cam")) * inverse_cols
+    full_gram = lax.psum(lax.psum(own_gram, "light"), ("pix", "cam")) * inverse_cols
     gram_rows = lax.dynamic_slice_in_dim(full_gram, position * light_rows, light_rows, 0)
     basis_now = start_basis
     for iteration in range(ITERS):

time: 582 us -> 678 us (1.16)
  waiting for transfers between devices: 201 us -> 297 us
    psum x1 -> x2, waiting for transfers between devices: 126 us -> 221 us  [the longest x1 154 us: per_device(): lax.psum(own_gram, 'light')]
  transfers between devices with their start and end apart: 2 -> 3, of which waited for: 2 -> 3; matrix products, arithmetic and copies ran while one was open for 3% -> 2% of each run, Pallas kernels for 0% -> 0%
where the time goes in v1:
time: 678 us; the launch traced here: 669 us
  waiting for transfers between devices  297 us (44%)
  blocking collectives  221 us (33%)
  local copies, waits for them, and re-layouts  61.5 us (9%)
  other arithmetic  45.7 us (7%)
  matrix products  28.8 us (4%)
  between operations  14.1 us (2%)
    all_to_all x1, blocking collectives, per_device(): lax.all_to_all(reflectance, 'light', split_axis=2, concat_axis=0, tiled=T...  192 us
    psum x1, waiting for transfers between devices, per_device(): lax.psum(own_gram, 'light')  154 us
    reduce_scatter x1, waiting for transfers between devices, per_device(): lax.psum_scatter(lax.dot_general(rounded, fibers, (((0,), (0,)), ((), ())...  76.3 us
    psum x1, waiting for transfers between devices, per_device(): lax.psum(lax.psum(own_gram, 'light'), ('pix', 'cam')) * inverse_cols  66.9 us
    unnamed x7, local copies, waits for them, and re-layouts  45.2 us
    all_gather x2, blocking collectives, per_device(): lax.all_gather(image_rows.astype(jnp.bfloat16), 'light', axis=0, tiled=True)  28.8 us
    another operation x6, other arithmetic, orthonormal(): factor = jnp.linalg.cholesky(inner_gram)  24.8 us
    another operation x4, other arithmetic, orthonormal(): lax.linalg.triangular_solve(factor, image_full, left_side=False, lower=Tr...  20.9 us
  transfers between devices with their start and end apart: 3, of which 3 were waited for; matrix products, arithmetic and copies ran while one was open for 2% of the time, Pallas kernels for 0%

profile of v1, /device:TPU:0, one launch (start us, length us, event | category | flops | bytes accessed | tf_op | source)
XLA Modules:
  0.0 669.2 jit_solution(13309129927128171678)
XLA Ops:
  7.2 13.4 %copy.16 = bf16[256,16,1024]{0,1,2:T(8,128)(2,1)} copy(bf16[256,16,1024]{2,1,0:T(8,128)(2,1)} %param.5) | data formatting | bytes 16777216 | tf_op args[0]
  20.7 192.2 %all_to_all.15 = bf16[256,16,1024]{0,1,2:T(8,128)(2,1)} all-to-all(bf16[256,16,1024]{0,1,2:T(8,128)(2,1)} %copy.16), channel_id=1, replica_groups=mesh['light'=4,'pix'=4,'cam'=2] {'light'}, dimensions={2} | all-to-all | bytes 16777216 | tf_op jit(solution)/shard_map/all_to_all | solution.py:31
  212.9 16.0 %copy.17 = bf16[256,16,4,256]{3,1,0,2:T(8,128)(2,1)} copy(bf16[256,16,4,256]{0,1,3,2:T(8,128)(2,1)} %bitcast.43) | data formatting | bytes 16777216 | tf_op jit(solution)/shard_map/all_to_all | solution.py:31
  228.9 12.2 %copy.21 = bf16[128,8,16,256]{3,1,2,0:T(8,128)(2,1)} copy(bf16[128,8,16,256]{3,2,1,0:T(8,128)(2,1)} %bitcast.44) | data formatting | bytes 16777216
  241.1 16.0 %fusion.17 = f32[1024,1024]{1,0:T(8,128)} fusion(bf16[1024,4096]{1,0:T(8,128)(2,1)} %bitcast.45), kind=kOutput, calls=%fused_computation.33 | convolution fusion | flops 8589934592 | bytes 12582912 | tf_op jit(solution)/shard_map/dot_general | solution.py:33
  257.2 154.2 %all-reduce.3.cloned.1.call-done = f32[1024,1024]{1,0:T(8,128)} async-done(((f32[1024,1024]{1,0:T(8,128)}), f32[1024,1024]{1,0:T(8,128)}) %all-reduce.3.cloned.1.call-update) | async-done | bytes 4194320 | tf_op jit(solution)/shard_map/psum | solution.py:36
  411.9 15.6 %copy.22 = bf16[32,8,16,1024]{3,1,2,0:T(8,128)(2,1)} copy(bf16[32,8,16,1024]{3,2,1,0:T(8,128)(2,1)} %bitcast.41) | data formatting | bytes 16777216
  427.6 66.9 %all-reduce.5.cloned.1.call-done = f32[1024,1024]{1,0:T(8,128)} async-done(((f32[1024,1024]{1,0:T(8,128)}), f32[1024,1024]{1,0:T(8,128)}) %all-reduce.5.cloned.1.call-update) | async-done | bytes 4194320 | tf_op jit(solution)/shard_map/psum | solution.py:36
  494.5 2.2 convolution_convert_fusion.2
  496.7 14.1 %all_gather.6 = bf16[1024,128]{1,0:T(8,128)(2,1)S(1)} all-gather(bf16[256,128]{1,0:T(8,128)(2,1)S(1)} %convolution_convert_fusion.2), channel_id=1, replica_groups=mesh['light'=4,'pix'=4,'cam'=2] {'light'}, dimensions={0}, use_global_device_ids=true | all-gather | bytes 327680 | tf_op jit(solution)/shard_map/all_gather | solution.py:46
  511.2 11.7 %cholesky.44 = f32[128,128]{1,0:T(8,128)S(1)} custom-call(f32[128,128]{1,0:T(8,128)S(1)} %fusion.9), custom_call_target="Cholesky" | custom-call | tf_op jit(solution)/shard_map/jit(cholesky)/cholesky | solution.py:16
  522.9 0.6 compare_reduce_fusion.1
  523.6 0.7 fusion.4
  524.3 9.8 %custom-call.6 = f32[1,128,128]{1,2,0:T(8,128)S(1)} custom-call(f32[1,128,128]{2,1,0:T(8,128)S(1)} %fusion.4), custom_call_target="InvertDiagBlocksLowerTriangular" | custom-call | tf_op jit(solution)/shard_map/triangular_solve/custom-call.0 | solution.py:17
  534.7 2.2 convolution_convert_fusion.1
  536.9 14.7 %all_gather.7 = bf16[1024,128]{1,0:T(8,128)(2,1)S(1)} all-gather(bf16[256,128]{1,0:T(8,128)(2,1)S(1)} %convolution_convert_fusion.1), channel_id=1, replica_groups=mesh['light'=4,'pix'=4,'cam'=2] {'light'}, dimensions={0}, use_global_device_ids=true | all-gather | bytes 327680 | tf_op jit(solution)/shard_map/all_gather | solution.py:46
  552.0 11.7 %cholesky.55 = f32[128,128]{1,0:T(8,128)S(1)} custom-call(f32[128,128]{1,0:T(8,128)S(1)} %fusion.7), custom_call_target="Cholesky" | custom-call | tf_op jit(solution)/shard_map/jit(cholesky)/cholesky | solution.py:16
  563.7 0.6 compare_reduce_fusion
  564.4 0.7 fusion.5
  565.0 9.8 %custom-call.7 = f32[1,128,128]{1,2,0:T(8,128)S(1)} custom-call(f32[1,128,128]{2,1,0:T(8,128)S(1)} %fusion.5), custom_call_target="InvertDiagBlocksLowerTriangular" | custom-call | tf_op jit(solution)/shard_map/triangular_solve/custom-call.0 | solution.py:17
  575.5 6.6 convolution_convert_fusion
  582.2 0.8 copy.20
  582.9 76.3 %reduce-scatter.2.cloned.1.call-done = bf16[32,16384]{1,0:T(8,128)(2,1)} async-done(((bf16[128,16384]{1,0:T(8,128)(2,1)}), bf16[32,16384]{1,0:T(8,128)(2,1)}) %reduce-scatter.2.cloned.1.call-update) | async-done | bytes 1048592 | tf_op jit(solution)/shard_map/reduce_scatter | solution.py:53
  659.3 3.2 copy.23
  (19 shorter events, 2.7 us)
Async XLA Ops:
  7.2 487.3 %copy-start = (f32[1024,128]{1,0:T(8,128)S(1)}, f32[1024,128]{1,0:T(8,128)}, u32[]{:S(2)}) copy-start(f32[1024,128]{1,0:T(8,128)} %param.6) | copy-start | bytes 1572868
  7.2 404.2 %all-reduce.3.cloned.1.call-start = ((), (), s32[]{:S(2)}) async-start(), calls=%async_computation.2 | async-start | bytes 8388608 | tf_op jit(solution)/shard_map/psum | solution.py:36
  257.1 237.3 %all-reduce.5.cloned.1.call-start = ((), (), s32[]{:S(2)}) async-start(), calls=%async_computation.3 | async-start | bytes 8388608 | tf_op jit(solution)/shard_map/psum | solution.py:36
  411.4 247.8 %reduce-scatter.2.cloned.1.call-start = ((), (), s32[]{:S(2)}) async-start(), calls=%async_computation.4 | async-start | bytes 5242880 | tf_op jit(solution)/shard_map/reduce_scatter | solution.py:53
Sparse Core Ops, SparseCore 0:
  257.3 154.0 all-reduce.2
  414.7 79.7 all-reduce.4
  582.3 76.9 reduce-scatter.1
